TPU v7x, 512 devices: a whole 4x8x8 slice. The times are simulated.
512 devices in a mesh: dof: 64 (over z, y_lo, core), real: 8 (over y_hi, x).
Axes of the slice: x: 4, y: 8 (y_hi: 2, y_lo: 4; y = y_hi * 4 + y_lo), z: 8, core: 2. Of those that a mesh axis runs over, the one named last changes fastest.
Arguments:
- mode_panel: bfloat16 [131072, 512], P('dof'), may hold values from -0.31445312 to 0.31445312
- stiff_blocks: bfloat16 [1024, 5, 128, 128], P('dof'), as said below
- stiff_cols: int32 [1024, 5], P('dof'), may hold values from 0 to 1023, as said below
- row_blade: int32 [131072], P('dof'), may hold values from 0 to 3, as said below
- adjusted_values: float32 [512], replicated, may hold values from 4 to 24
- deviations: float32 [128, 4], P('dof'), may hold values from -0.05 to 0.05
- start_block: float32 [512, 128], P('real'), may hold values from -6 to 6
Outputs:
- projected: float32 [4, 512, 512], P(None, 'real')
- subspace: float32 [128, 512, 128], P('dof', 'real')
Inputs may be any that keep to these rules, and one draw needn't show every extreme that they name: `stiff_cols`: each block row's 5 entries are, in some order, the block row itself and the block rows two and one before and one and two after it; where one of those lies outside the grid or in another blade's rows, the block row itself stands in. `stiff_blocks`: the stiffness is symmetric and couples no two blades: the block of block row g at column c is the transpose of the block of block row c at column g, diagonal blocks are symmetric, and stand-in blocks are zero. `row_blade`: block row g belongs to the blade numbered ((g + 8) // 256) mod 4 under a fixed relabelling of the blades; so each blade owns a run of 32768 neighbouring rows, except one blade, which owns the first 31744 rows and the last 1024 rows.
All inputs are finite; a program needn't handle non-finite values.
Results may differ from a plain program's by a relative error of at most 0.003.
Values may be sent and summed in bfloat16 or wider, within the bound.
No kernel may reach another device: no remote copies, remote signals or barrier semaphores. Data moves between devices by JAX's collectives and lax.ppermute only.
A program may use at most 64 MiB of HBM per device.

v0:
```python
import jax
import jax.numpy as jnp
from jax import lax
from jax.sharding import PartitionSpec as P

ADJUSTED_MODES = 512
NBLADE = 4
STEPS = 2
highest_accuracy = lax.Precision.HIGHEST


def with_halo(block, sides, width):
    for axis, dim in sides:
        count = lax.axis_size(axis)
        forward = [(i, i + 1) for i in range(count - 1)]
        backward = [(target, source) for source, target in forward]
        low = lax.ppermute(
            lax.slice_in_dim(block, block.shape[dim] - width, None, axis=dim), axis, forward
        )
        high = lax.ppermute(lax.slice_in_dim(block, 0, width, axis=dim), axis, backward)
        block = jnp.concatenate([low, block, high], axis=dim)
    return block


def multiply_by_blocks(ext_blocks, blocks, columns):
    number = blocks.shape[0]
    size = blocks.shape[2]
    mode_count = ext_blocks.shape[2]
    row_totals = jnp.zeros((number, size, mode_count), jnp.float32)
    for slot_index in range(blocks.shape[1]):
        picked = jnp.take(ext_blocks, columns[:, slot_index], axis=0)
        row_totals = row_totals + jnp.einsum(
            "gab,gbm->gam", blocks[:, slot_index], picked, preferred_element_type=jnp.float32
        )
    return row_totals.reshape(number * size, mode_count).astype(jnp.bfloat16)


def add_projection(portion, offset, mode_panel, row_blade, col_start, owned_rows):
    number = portion.shape[0]
    left_rows = lax.dynamic_slice(mode_panel, (offset, col_start), (number, owned_rows))
    stacked = jnp.concatenate(
        [
            jnp.where((row_blade == blade_index)[:, None], left_rows, jnp.zeros_like(left_rows))
            for blade_index in range(NBLADE)
        ],
        axis=1,
    )
    return lax.dot_general(
        stacked, portion, (((0,), (0,)), ((), ())), preferred_element_type=jnp.float32
    )


def inverse_factor(inner_product_matrix):
    factor = jnp.linalg.cholesky(inner_product_matrix)
    identity = jnp.broadcast_to(
        jnp.eye(inner_product_matrix.shape[-1], dtype=inner_product_matrix.dtype),
        inner_product_matrix.shape,
    )
    return lax.linalg.triangular_solve(factor, identity, left_side=True, lower=True)


def normalize_parts(present_image):
    partial_inner_products = jnp.einsum(
        "eox,eol->exl", present_image, present_image, precision=highest_accuracy
    )
    inner_product_matrix = lax.psum(partial_inner_products, "real") / ADJUSTED_MODES
    inverse = inverse_factor(inner_product_matrix)
    return jnp.einsum("zjs,zts->zjt", present_image, inverse, precision=highest_accuracy)


def on_device(
    mode_panel, stiff_blocks, stiff_cols, row_blade, adjusted_values, deviations, start_block
):
    real_count = lax.axis_size("real")
    owner_index = lax.axis_index("real")
    mode_count = mode_panel.shape[1]
    owned_rows = mode_count // real_count
    block_size = stiff_blocks.shape[2]
    shard_blocks = stiff_blocks.shape[0]
    col_start = owner_index * owned_rows
    extended = with_halo(mode_panel, (("dof", 0),), 2 * block_size)
    ext_blocks = extended.reshape(shard_blocks + 4, block_size, mode_count)
    local_cols = stiff_cols - lax.axis_index("dof") * shard_blocks + 2
    stiff_image = multiply_by_blocks(ext_blocks, stiff_blocks, local_cols)
    blade_parts = add_projection(
        stiff_image, jnp.zeros((), jnp.int32), mode_panel, row_blade, col_start, owned_rows
    )
    summed = lax.psum(blade_parts, "dof")
    projected = summed.reshape(NBLADE, owned_rows, mode_count)
    row_ids = jnp.arange(owned_rows, dtype=jnp.int32) + col_start
    own_values = lax.dynamic_slice_in_dim(adjusted_values, col_start, owned_rows, 0)
    diagonal_part = jnp.where(
        jnp.arange(mode_count, dtype=jnp.int32)[None, :] == row_ids[:, None],
        own_values[:, None],
        jnp.zeros((), jnp.float32),
    )
    realizations = deviations.shape[0]
    subspace_width = start_block.shape[1]
    reduced = (
        jnp.einsum("zb,bjm->zjm", deviations, projected, precision=highest_accuracy)
        + diagonal_part[None]
    )
    current = jnp.broadcast_to(start_block[None], (realizations, owned_rows, subspace_width))
    for iteration in range(STEPS):
        present_image = jnp.einsum(
            "zjk,zks->zjs",
            reduced,
            lax.all_gather(current, "real", axis=1, tiled=True),
            precision=highest_accuracy,
        )
        current = normalize_parts(present_image)
    return (projected, current)


def solution(mesh):
    in_specs = (
        P("dof", None),
        P("dof", None, None, None),
        P("dof", None),
        P("dof"),
        P(),
        P("dof", None),
        P("real", None),
    )
    out_specs = (P(None, "real", None), P("dof", "real", None))
    return jax.shard_map(
        on_device, mesh=mesh, in_specs=in_specs, out_specs=out_specs, check_vma=False
    )
```

profile of v0, /device:TPU:64, one launch (start us, length us, event | category | flops | bytes accessed | tf_op | source)
XLA Modules:
  0.0 967.4 jit_solution(17578840527042316968)
XLA Ops:
  7.2 1.1 fusion.60
  8.3 1.9 collective-permute-start
  10.2 6.3 collective-permute-start.1
  18.0 5.4 broadcast_select_fusion.3
  24.4 2.0 gather_fusion.2
  26.4 2.0 gather_fusion.1
  28.4 2.0 gather_fusion.3
  30.4 2.0 gather_fusion.4
  32.4 2.0 gather_fusion
  34.5 2.7 fusion.3
  40.0 0.8 copy-done.4
  42.4 1.6 add_convert_fusion
  44.0 1.3 fusion.15
  45.3 1.1 copy.27
  46.6 44.8 %all_gather.8 = f32[512,128]{1,0:T(8,128)S(1)} all-gather(f32[64,128]{1,0:T(8,128)S(1)} %copy-done.12), channel_id=2, replica_groups=mesh['dof'=64,'real'=8] {'real'}, dimensions={0}, use_global_device_ids=true | all-gather | bytes 294912 | tf_op jit(solution)/shard_map/all_gather | solution.py:108
  91.5 492.6 %all-reduce.4.cloned.1.call-done = f32[4,64,512]{2,0,1:T(4,128)} async-done(((f32[4,64,512]{2,0,1:T(4,128)}), f32[4,64,512]{2,0,1:T(4,128)}) %all-reduce.4.cloned.1.call-update) | async-done | bytes 524304 | tf_op jit(solution)/shard_map/psum | solution.py:88
  584.2 2.1 fusion.14
  586.7 1.0 fusion.61
  588.0 125.4 %all-reduce.6.cloned.1.call-done = f32[2,128,128]{1,2,0:T(8,128)} async-done(((f32[2,128,128]{1,2,0:T(8,128)}), f32[2,128,128]{1,2,0:T(8,128)}) %all-reduce.6.cloned.1.call-update) | async-done | bytes 131088 | tf_op jit(solution)/shard_map/psum | solution.py:66
  713.4 0.9 broadcast_multiply_fusion.1
  714.4 0.9 fusion.48
  715.4 23.5 %custom-call.8 = f32[2,128,128]{2,1,0:T(8,128)S(1)} custom-call(f32[2,128,128]{2,1,0:T(8,128)S(1)} %fusion.48), custom_call_target="Cholesky" | custom-call | tf_op jit(solution)/shard_map/jit(cholesky)/cholesky | solution.py:54
  739.1 19.7 %custom-call.9 = f32[2,1,128,128]{2,3,1,0:T(8,128)S(1)} custom-call(f32[2,1,128,128]{3,2,1,0:T(8,128)S(1)} %select_bitcast_fusion.1), custom_call_target="InvertDiagBlocksLowerTriangular" | custom-call | tf_op jit(solution)/shard_map/triangular_solve/custom-call.0 | solution.py:59
  759.5 45.8 %all_gather.7 = f32[2,512,128]{2,1,0:T(8,128)S(1)} all-gather(f32[2,64,128]{2,1,0:T(8,128)S(1)} %fusion.62), channel_id=1, replica_groups=mesh['dof'=64,'real'=8] {'real'}, dimensions={1}, use_global_device_ids=true | all-gather | bytes 589824 | tf_op jit(solution)/shard_map/all_gather | solution.py:108
  805.8 1.0 fusion.63
  806.9 1.0 copy.34
  807.8 106.3 %all-reduce.8.cloned.1.call-done = f32[2,128,128]{1,2,0:T(8,128)} async-done(((f32[2,128,128]{1,2,0:T(8,128)}), f32[2,128,128]{1,2,0:T(8,128)}) %all-reduce.8.cloned.1.call-update) | async-done | bytes 131088 | tf_op jit(solution)/shard_map/psum | solution.py:66
  914.1 0.9 broadcast_multiply_fusion
  915.1 0.9 fusion.45
  916.0 23.5 %custom-call.10 = f32[2,128,128]{2,1,0:T(8,128)S(1)} custom-call(f32[2,128,128]{2,1,0:T(8,128)S(1)} %fusion.45), custom_call_target="Cholesky" | custom-call | tf_op jit(solution)/shard_map/jit(cholesky)/cholesky | solution.py:54
  939.8 19.7 %custom-call.11 = f32[2,1,128,128]{2,3,1,0:T(8,128)S(1)} custom-call(f32[2,1,128,128]{3,2,1,0:T(8,128)S(1)} %select_bitcast_fusion), custom_call_target="InvertDiagBlocksLowerTriangular" | custom-call | tf_op jit(solution)/shard_map/triangular_solve/custom-call.0 | solution.py:59
  959.8 1.0 fusion.64
  (62 shorter events, 10.0 us)
Async XLA Ops:
  7.2 577.0 %copy-start = (f32[2,4]{1,0:T(2,128)S(1)}, f32[2,4]{1,0:T(2,128)}, u32[]{:S(2)}) copy-start(f32[2,4]{1,0:T(2,128)} %param.17) | copy-start | bytes 100
  7.2 577.0 %all-reduce.4.cloned.1.call-start = ((), (), s32[]{:S(2)}) async-start(), calls=%async_computation | async-start | bytes 1048576 | tf_op jit(solution)/shard_map/psum | solution.py:88
  8.3 15.9 %collective-permute-start = (bf16[256,512]{1,0:T(8,128)(2,1)S(1)}, bf16[256,512]{1,0:T(8,128)(2,1)S(1)}, u32[]{:S(2)}, u32[]{:S(2)}) collective-permute-start(bf16[256,512]{1,0:T(8,128)(2,1)S(1)} %get-tuple-element.23), channel_id=1, source_target_pairs={{0,8},{8,16},{16,24},{24,32},{32,40},{40,48},{48,56},{56,64},{64,7... | collective-permute-start | bytes 786440 | tf_op jit(solution)/shard_map/ppermute | solution.py:17
  10.2 14.0 %collective-permute-start.1 = (bf16[256,512]{1,0:T(8,128)(2,1)S(1)}, bf16[256,512]{1,0:T(8,128)(2,1)S(1)}, u32[]{:S(2)}, u32[]{:S(2)}) collective-permute-start(bf16[256,512]{1,0:T(8,128)(2,1)S(1)} %get-tuple-element.24), channel_id=1, source_target_pairs={{8,0},{16,8},{24,16},{32,24},{40,32},{48,40},{56,48},{64,56},{72,6... | collective-permute-start | bytes 786440 | tf_op jit(solution)/shard_map/ppermute | solution.py:20
  18.0 6.2 copy-start.5
  34.5 2.7 copy-start.3
  34.5 3.2 copy-start.6
  37.6 1.6 copy-start.2
  39.2 1.6 copy-start.4
  40.8 1.6 copy-start.1
  42.4 1.6 copy-start.8
  42.4 1.6 copy-start.9
  42.4 1.6 copy-start.10
  42.4 1.6 copy-start.11
  44.0 2.5 copy-start.12
  46.5 666.9 %all-reduce.6.cloned.1.call-start = ((), (), s32[]{:S(2)}) async-start(), calls=%async_computation.1 | async-start | bytes 262144 | tf_op jit(solution)/shard_map/psum | solution.py:66
  586.7 220.2 %copy-start.7 = (f32[4,64,512]{2,0,1:T(4,128)S(1)}, f32[4,64,512]{2,0,1:T(4,128)}, u32[]{:S(2)}) copy-start(f32[4,64,512]{2,0,1:T(4,128)} %all-reduce.4.cloned.1.call-done) | copy-start | bytes 1572868
  587.8 326.3 %all-reduce.8.cloned.1.call-start = ((), (), s32[]{:S(2)}) async-start(), calls=%async_computation.2 | async-start | bytes 262144 | tf_op jit(solution)/shard_map/psum | solution.py:66
Sparse Core Ops, SparseCore 0:
  46.6 537.4 all-reduce.3
  587.9 125.4 all-reduce.5
  807.0 107.0 all-reduce.7
where the time goes:
time: 968 us; the launch traced here: 967 us
  waiting for transfers between devices  724 us (75%)
  other arithmetic  97.6 us (10%)
  blocking collectives  90.7 us (9%)
  local copies, waits for them, and re-layouts  17.1 us (2%)
  matrix products  15 us (2%)
  between operations  14.1 us (1%)
    psum x1, waiting for transfers between devices, on_device(): summed = lax.psum(blade_parts, 'dof')  493 us
    psum x2, waiting for transfers between devices, normalize_parts(): lax.psum(partial_inner_products, 'real') / ADJUSTED_MODES  232 us
    all_gather x2, blocking collectives, on_device(): lax.all_gather(current, 'real', axis=1, tiled=True)  90.7 us
    another operation x7, other arithmetic, inverse_factor(): factor = jnp.linalg.cholesky(inner_product_matrix)  47.2 us
    another operation x5, other arithmetic, inverse_factor(): lax.linalg.triangular_solve(factor, identity, left_side=True, lower=True)  39.6 us
  transfers between devices with their start and end apart: 5, of which 3 were waited for; matrix products, arithmetic and copies ran while one was open for 1% of the time, Pallas kernels for 0%

commit v1 on v0

--- a/solution.py
+++ b/solution.py
@@ -71,6 +71,10 @@
 def on_device(
     mode_panel, stiff_blocks, stiff_cols, row_blade, adjusted_values, deviations, start_block
 ):
+
+    def supply_all_view(w_in):
+        return lax.all_gather(w_in, "dof").sum(axis=0)
+
     real_count = lax.axis_size("real")
     owner_index = lax.axis_index("real")
     mode_count = mode_panel.shape[1]
@@ -85,7 +89,7 @@
     blade_parts = add_projection(
         stiff_image, jnp.zeros((), jnp.int32), mode_panel, row_blade, col_start, owned_rows
     )
-    summed = lax.psum(blade_parts, "dof")
+    summed = supply_all_view(blade_parts)
     projected = summed.reshape(NBLADE, owned_rows, mode_count)
     row_ids = jnp.arange(owned_rows, dtype=jnp.int32) + col_start
     own_values = lax.dynamic_slice_in_dim(adjusted_values, col_start, owned_rows, 0)

time: 968 us -> 628 us (0.65)
  waiting for transfers between devices: 724 us -> 373 us
  other arithmetic: 97.6 us -> 111 us
    psum x1 -> x0, waiting for transfers between devices: 493 us -> none  [on_device(): summed = lax.psum(blade_parts, 'dof')]
    all_gather x0 -> x1, waiting for transfers between devices: none -> 152 us  [supply_all_view(): return lax.all_gather(w_in, 'dof').sum(axis=0)]
    reduce_sum x0 -> x1, other arithmetic: none -> 12.1 us  [supply_all_view(): return lax.all_gather(w_in, 'dof').sum(axis=0)]
    psum x2, waiting for transfers between devices: 232 us -> 221 us  [normalize_parts(): lax.psum(partial_inner_products, 'real') / ADJUSTED_MODES]
where the time goes in v1:
time: 628 us; the launch traced here: 627 us
  waiting for transfers between devices  373 us (59%)
  other arithmetic  111 us (18%)
  blocking collectives  91.1 us (15%)
  matrix products  15.1 us (2%)
  local copies, waits for them, and re-layouts  15 us (2%)
  between operations  14.1 us (2%)
  starting transfers between devices  8.56 us (1%)
    psum x2, waiting for transfers between devices, normalize_parts(): lax.psum(partial_inner_products, 'real') / ADJUSTED_MODES  221 us
    all_gather x1, waiting for transfers between devices, supply_all_view(): return lax.all_gather(w_in, 'dof').sum(axis=0)  152 us
    all_gather x2, blocking collectives, on_device(): lax.all_gather(current, 'real', axis=1, tiled=True)  91.1 us
    another operation x7, other arithmetic, inverse_factor(): factor = jnp.linalg.cholesky(inner_product_matrix)  47.2 us
    another operation x5, other arithmetic, inverse_factor(): lax.linalg.triangular_solve(factor, identity, left_side=True, lower=True)  39.6 us
  transfers between devices with their start and end apart: 5, of which 3 were waited for; matrix products, arithmetic and copies ran while one was open for 1% of the time, Pallas kernels for 0%

profile of v1, /device:TPU:64, one launch (start us, length us, event | category | flops | bytes accessed | tf_op | source)
XLA Modules:
  0.0 627.3 jit_solution(8035535605177183888)
XLA Ops:
  7.2 1.1 fusion.61
  8.3 1.9 collective-permute-start
  10.2 6.3 %collective-permute-start.1 = (bf16[256,512]{1,0:T(8,128)(2,1)S(1)}, bf16[256,512]{1,0:T(8,128)(2,1)}, u32[]{:S(2)}, u32[]{:S(2)}) collective-permute-start(bf16[256,512]{1,0:T(8,128)(2,1)S(1)} %get-tuple-element.20), channel_id=1, source_target_pairs={{8,0},{16,8},{24,16},{32,24},{40,32},{48,40},{56,48},{64,56},{72,6... | collective-permute-start | bytes 786440 | tf_op jit(solution)/shard_map/ppermute | solution.py:20
  18.0 5.3 broadcast_select_fusion.3
  23.4 1.1 pad_maximum_fusion
  24.5 2.0 gather_fusion.2
  26.5 2.0 gather_fusion.1
  28.6 2.0 gather_fusion.3
  30.5 2.0 gather_fusion.4
  32.6 2.0 gather_fusion
  34.6 2.7 fusion.3
  40.1 0.8 copy-done.4
  42.6 1.6 add_convert_fusion
  44.2 2.1 fusion.15
  47.1 45.2 %all_gather.16 = f32[512,128]{1,0:T(8,128)S(1)} all-gather(f32[64,128]{1,0:T(8,128)S(1)} %copy-done.11), channel_id=2, replica_groups=mesh['dof'=64,'real'=8] {'real'}, dimensions={0}, use_global_device_ids=true | all-gather | bytes 294912 | tf_op jit(solution)/shard_map/all_gather | solution.py:112
  92.4 151.8 %all-gather.3.cloned.1.call-done = f32[16384,512]{1,0:T(8,128)} async-done(((f32[256,512]{1,0:T(8,128)}), f32[16384,512]{1,0:T(8,128)}) %all-gather.3.cloned.1.call-update) | async-done | bytes 33554448 | tf_op jit(solution)/shard_map/all_gather | solution.py:76
  244.2 12.1 %reduce_sum.9 = f32[256,512]{1,0:T(8,128)S(1)} reduce(f32[64,256,512]{2,1,0:T(8,128)} %bitcast.84, f32[]{:T(128)} %constant.71.clone.1), dimensions={0}, to_apply=%region_0.0 | reduce | flops 8257536 | bytes 34078724 | tf_op jit(solution)/shard_map/reduce_sum | solution.py:76
  256.3 1.3 fusion.14
  258.1 1.1 fusion.62
  259.5 113.8 %all-reduce.3.cloned.1.call-done = f32[2,128,128]{1,2,0:T(8,128)} async-done(((f32[2,128,128]{1,2,0:T(8,128)}), f32[2,128,128]{1,2,0:T(8,128)}) %all-reduce.3.cloned.1.call-update) | async-done | bytes 131088 | tf_op jit(solution)/shard_map/psum | solution.py:66
  373.3 0.9 broadcast_multiply_fusion.1
  374.4 0.9 fusion.49
  375.3 23.5 %custom-call.8 = f32[2,128,128]{2,1,0:T(8,128)S(1)} custom-call(f32[2,128,128]{2,1,0:T(8,128)S(1)} %fusion.49), custom_call_target="Cholesky" | custom-call | tf_op jit(solution)/shard_map/jit(cholesky)/cholesky | solution.py:54
  399.0 19.7 %custom-call.9 = f32[2,1,128,128]{2,3,1,0:T(8,128)S(1)} custom-call(f32[2,1,128,128]{3,2,1,0:T(8,128)S(1)} %select_bitcast_fusion.1), custom_call_target="InvertDiagBlocksLowerTriangular" | custom-call | tf_op jit(solution)/shard_map/triangular_solve/custom-call.0 | solution.py:59
  419.4 45.8 %all_gather.15 = f32[2,512,128]{2,1,0:T(8,128)S(1)} all-gather(f32[2,64,128]{2,1,0:T(8,128)S(1)} %fusion.63), channel_id=1, replica_groups=mesh['dof'=64,'real'=8] {'real'}, dimensions={1}, use_global_device_ids=true | all-gather | bytes 589824 | tf_op jit(solution)/shard_map/all_gather | solution.py:112
  465.7 1.1 fusion.64
  466.8 107.2 %all-reduce.5.cloned.1.call-done = f32[2,128,128]{1,2,0:T(8,128)} async-done(((f32[2,128,128]{1,2,0:T(8,128)}), f32[2,128,128]{1,2,0:T(8,128)}) %all-reduce.5.cloned.1.call-update) | async-done | bytes 131088 | tf_op jit(solution)/shard_map/psum | solution.py:66
  574.0 0.9 broadcast_multiply_fusion
  575.1 0.9 fusion.46
  576.0 23.5 %custom-call.10 = f32[2,128,128]{2,1,0:T(8,128)S(1)} custom-call(f32[2,128,128]{2,1,0:T(8,128)S(1)} %fusion.46), custom_call_target="Cholesky" | custom-call | tf_op jit(solution)/shard_map/jit(cholesky)/cholesky | solution.py:54
  599.7 19.7 %custom-call.11 = f32[2,1,128,128]{2,3,1,0:T(8,128)S(1)} custom-call(f32[2,1,128,128]{3,2,1,0:T(8,128)S(1)} %select_bitcast_fusion), custom_call_target="InvertDiagBlocksLowerTriangular" | custom-call | tf_op jit(solution)/shard_map/triangular_solve/custom-call.0 | solution.py:59
  619.8 1.0 fusion.65
  (59 shorter events, 9.8 us)
Async XLA Ops:
  7.2 249.2 %copy-start = (f32[2,4]{1,0:T(2,128)S(1)}, f32[2,4]{1,0:T(2,128)}, u32[]{:S(2)}) copy-start(f32[2,4]{1,0:T(2,128)} %param.17) | copy-start | bytes 100
  7.2 237.0 %all-gather.3.cloned.1.call-start = ((), (), s32[]{:S(2)}) async-start(), calls=%async_computation.2 | async-start | bytes 34078720 | tf_op jit(solution)/shard_map/all_gather | solution.py:76
  8.3 15.1 %collective-permute-start = (bf16[256,512]{1,0:T(8,128)(2,1)S(1)}, bf16[256,512]{1,0:T(8,128)(2,1)S(1)}, u32[]{:S(2)}, u32[]{:S(2)}) collective-permute-start(bf16[256,512]{1,0:T(8,128)(2,1)S(1)} %get-tuple-element.19), channel_id=1, source_target_pairs={{0,8},{8,16},{16,24},{24,32},{32,40},{40,48},{48,56},{56,64},{64,7... | collective-permute-start | bytes 786440 | tf_op jit(solution)/shard_map/ppermute | solution.py:17
  10.2 13.2 %collective-permute-start.1 = (bf16[256,512]{1,0:T(8,128)(2,1)S(1)}, bf16[256,512]{1,0:T(8,128)(2,1)}, u32[]{:S(2)}, u32[]{:S(2)}) collective-permute-start(bf16[256,512]{1,0:T(8,128)(2,1)S(1)} %get-tuple-element.20), channel_id=1, source_target_pairs={{8,0},{16,8},{24,16},{32,24},{40,32},{48,40},{56,48},{64,56},{72,6... | collective-permute-start | bytes 786440 | tf_op jit(solution)/shard_map/ppermute | solution.py:20
  18.0 5.4 copy-start.5
  34.6 2.7 copy-start.3
  34.6 3.2 copy-start.6
  37.8 1.6 copy-start.2
  39.4 1.6 copy-start.4
  41.0 1.6 copy-start.1
  42.5 1.6 copy-start.8
  42.5 1.6 copy-start.9
  42.5 1.6 copy-start.10
  44.1 2.9 copy-start.11
  46.2 327.1 %all-reduce.3.cloned.1.call-start = ((), (), s32[]{:S(2)}) async-start(), calls=%async_computation | async-start | bytes 262144 | tf_op jit(solution)/shard_map/psum | solution.py:66
  256.3 208.9 %copy-start.7 = (f32[256,512]{1,0:T(8,128)}, f32[256,512]{1,0:T(8,128)S(1)}, u32[]{:S(2)}) copy-start(f32[256,512]{1,0:T(8,128)S(1)} %reduce_sum.9) | copy-start | bytes 1572868
  259.2 314.8 %all-reduce.5.cloned.1.call-start = ((), (), s32[]{:S(2)}) async-start(), calls=%async_computation.1 | async-start | bytes 262144 | tf_op jit(solution)/shard_map/psum | solution.py:66
Sparse Core Ops, SparseCore 0:
  46.4 197.8 all-gather.2
  259.3 113.9 all-reduce.2
  466.9 107.0 all-reduce.4
